TPU v7x, 512 devices: a whole 4x4x16 slice. The times are simulated.
512 devices in a mesh: dp: 32 (over x, y, core), expert: 16 (over z).
Axes of the slice: x: 4, y: 4, z: 16, core: 2. Of those that a mesh axis runs over, the one named last changes fastest.
Arguments:
- tokens: bfloat16 [4096, 2048], P('dp', 'expert'), may hold values from -6 to 6
- cotangent: bfloat16 [4096, 2048], P('dp', 'expert'), may hold values from -6 to 6
- expert_ids: int32 [4096, 8], P('dp'), may hold values from 0 to 127, all different within a row; in each aligned block of 128 rows (0 to 127, 128 to 255, ...) at most 16 rows name the same one
- gate_weights: float32 [4096, 8], P('dp'), may hold values from 0.05 to 1
- w_gate: bfloat16 [512, 192, 2048], P(('dp', 'expert')), may hold values from -0.125 to 0.125
- w_up: bfloat16 [512, 192, 2048], P(('dp', 'expert')), may hold values from -0.125 to 0.125
- w_down: bfloat16 [512, 192, 2048], P(('dp', 'expert')), may hold values from -0.21875 to 0.21875
Outputs:
- layer_out: bfloat16 [4096, 2048], P('dp', 'expert')
- grad_tokens: bfloat16 [4096, 2048], P('dp', 'expert')
- grad_gates: float32 [4096, 8], P('dp')
- grad_w_gate: bfloat16 [512, 192, 2048], P(('dp', 'expert'))
- grad_w_up: bfloat16 [512, 192, 2048], P(('dp', 'expert'))
- grad_w_down: bfloat16 [512, 192, 2048], P(('dp', 'expert'))
Inputs may be any that keep to these rules, and one draw needn't show every extreme that they name: `expert_ids`: each row names 8 different experts. In each aligned block of 128 rows (the rows of one index of dp) no expert is named by more than 16 rows, and in some block an expert is named by exactly 16 rows.
All inputs are finite; a program needn't handle non-finite values.
Results may differ from a plain program's by a relative error of at most 0.0064.
Values may be sent and summed in bfloat16 or wider, within the bound.
No kernel may reach another device: no remote copies, remote signals or barrier semaphores. Data moves between devices by JAX's collectives and lax.ppermute only.
A program may use at most 64 MiB of HBM per device.

v0:
```python
import jax
import jax.numpy as jnp
from jax import lax
from jax.sharding import PartitionSpec as P

SHARDS = 4


def silu_parts(preact):
    sigmoid_of = jax.nn.sigmoid(preact)
    activated = preact * sigmoid_of
    derivative = sigmoid_of * (1.0 + preact * (1.0 - sigmoid_of))
    return (activated, derivative)


def contract_last(first_op, second_op):
    return lax.dot_general(
        first_op, second_op, (((1,), (1,)), ((), ())), preferred_element_type=jnp.float32
    )


def contract_first(first_op, second_op):
    return lax.dot_general(
        first_op, second_op, (((0,), (0,)), ((), ())), preferred_element_type=jnp.float32
    )


def forward_rows(rows_x, gate_w, up_w, down_w):
    pre_gate = contract_last(rows_x, gate_w)
    pre_up = contract_last(rows_x, up_w)
    activated, derivative = silu_parts(pre_gate)
    hidden = (activated * pre_up).astype(jnp.bfloat16)
    return jnp.dot(hidden, down_w, preferred_element_type=jnp.float32).astype(jnp.bfloat16)


def backward_rows(rows_x, rows_do, gate_w, up_w, down_w):
    pre_gate = contract_last(rows_x, gate_w)
    pre_up = contract_last(rows_x, up_w)
    activated, derivative = silu_parts(pre_gate)
    hidden = (activated * pre_up).astype(jnp.bfloat16)
    d_hidden = contract_last(rows_do, down_w)
    d_pre_gate = (d_hidden * pre_up * derivative).astype(jnp.bfloat16)
    d_pre_up = (d_hidden * activated).astype(jnp.bfloat16)
    part_grad = (
        jnp.dot(d_pre_gate, gate_w, preferred_element_type=jnp.float32)
        + jnp.dot(d_pre_up, up_w, preferred_element_type=jnp.float32)
    ).astype(jnp.bfloat16)
    gradients = (
        contract_first(d_pre_gate, rows_x),
        contract_first(d_pre_up, rows_x),
        contract_first(hidden, rows_do),
    )
    return (part_grad, gradients)


def per_device(tokens, cotangent, expert_ids, gate_weights, w_gate, w_up, w_down):
    full_x, full_dy = (
        lax.all_gather(tokens, "expert", axis=1, tiled=True),
        lax.all_gather(cotangent, "expert", axis=1, tiled=True),
    )
    dp_count = lax.axis_size("dp")
    column_count = lax.axis_size("expert")
    column = lax.axis_index("expert")
    tok_count, chosen = expert_ids.shape
    features = full_x.shape[1]
    experts_all = dp_count * column_count // SHARDS
    capacity = min(tok_count, max(2, 2 * tok_count * chosen // experts_all))
    per_row = column_count // SHARDS
    assigned = tok_count * chosen
    flat_ids = expert_ids.reshape(-1)
    flat_gates = gate_weights.reshape(-1)
    owned_here = flat_ids % per_row == column // SHARDS
    target_row = flat_ids // per_row
    onehot = (
        (target_row[:, None] == jnp.arange(dp_count, dtype=jnp.int32)[None, :])
        & owned_here[:, None]
    ).astype(jnp.int32)
    rank_of = jnp.sum((jnp.cumsum(onehot, axis=0) - 1) * onehot, axis=1)
    target = jnp.where(owned_here, target_row * capacity + rank_of, dp_count * capacity)
    slot_src = (
        jnp.full((dp_count * capacity,), assigned, jnp.int32)
        .at[target]
        .set(jnp.arange(assigned, dtype=jnp.int32), mode="drop")
    )
    filled = slot_src < assigned
    safe_index = jnp.where(filled, slot_src, 0)
    slot_token = safe_index // chosen
    slot_gate = jnp.where(filled, flat_gates[safe_index], 0.0)
    slot_dy = full_dy[slot_token].astype(jnp.float32)
    send_x = jnp.where(filled[:, None], full_x[slot_token], jnp.zeros((), full_x.dtype)).reshape(
        dp_count, capacity, features
    )
    send_do = (
        (slot_gate[:, None] * slot_dy).astype(jnp.bfloat16).reshape(dp_count, capacity, features)
    )
    weights = (w_gate[0], w_up[0], w_down[0])
    recv_x = lax.all_to_all(send_x, "dp", split_axis=0, concat_axis=0, tiled=True)
    rows_x = recv_x.reshape(dp_count * capacity, features)
    expert_out = forward_rows(rows_x, *weights)
    back_out = lax.all_to_all(
        expert_out.reshape(dp_count, capacity, features),
        "dp",
        split_axis=0,
        concat_axis=0,
        tiled=True,
    )
    recv_do = lax.all_to_all(send_do, "dp", split_axis=0, concat_axis=0, tiled=True)
    rows_do = recv_do.reshape(dp_count * capacity, features)
    part_grad, gradients = backward_rows(rows_x, rows_do, *weights)
    back_grad = lax.all_to_all(
        part_grad.reshape(dp_count, capacity, features),
        "dp",
        split_axis=0,
        concat_axis=0,
        tiled=True,
    )
    width_now = back_out.shape[2]
    out_float = back_out.reshape(dp_count * capacity, width_now).astype(jnp.float32)
    grad_float = back_grad.reshape(dp_count * capacity, width_now).astype(jnp.float32)
    out_part = (
        jnp.zeros((tok_count, width_now), jnp.float32)
        .at[slot_token]
        .add(slot_gate[:, None] * out_float)
    )
    grad_part = jnp.zeros((tok_count, width_now), jnp.float32).at[slot_token].add(grad_float)
    gate_terms = jnp.sum(slot_dy * out_float, axis=1)
    gate_part = (
        jnp.zeros((assigned,), jnp.float32)
        .at[slot_src]
        .add(gate_terms, mode="drop")
        .reshape(tok_count, chosen)
    )
    out_slice, grad_slice = (
        lax.psum_scatter(out_part, "expert", scatter_dimension=1, tiled=True),
        lax.psum_scatter(grad_part, "expert", scatter_dimension=1, tiled=True),
    )
    grad_gates = lax.psum(gate_part, "expert")
    return (
        out_slice.astype(jnp.bfloat16),
        grad_slice.astype(jnp.bfloat16),
        grad_gates,
        gradients[0].astype(jnp.bfloat16)[None],
        gradients[1].astype(jnp.bfloat16)[None],
        gradients[2].astype(jnp.bfloat16)[None],
    )


def solution(mesh):
    placed = (
        P("dp", "expert"),
        P("dp", "expert"),
        P("dp", None),
        P("dp", None),
        P(("dp", "expert"), None, None),
        P(("dp", "expert"), None, None),
        P(("dp", "expert"), None, None),
    )
    return jax.shard_map(
        per_device,
        mesh=mesh,
        in_specs=placed,
        out_specs=(
            P("dp", "expert"),
            P("dp", "expert"),
            P("dp", None),
            P(("dp", "expert"), None, None),
            P(("dp", "expert"), None, None),
            P(("dp", "expert"), None, None),
        ),
        check_vma=False,
    )
```

profile of v0, /device:TPU:2, one launch (start us, length us, event | category | flops | bytes accessed | tf_op | source)
XLA Modules:
  0.0 339.8 jit_solution(6316037226412424405)
XLA Ops:
  7.2 0.0 copy-start
  7.2 0.9 copy.13
  8.0 0.1 reshape.230
  8.1 0.1 reshape.229
  8.2 0.1 reshape.228
  8.4 9.0 %reduce-window.6 = s32[32,8,128]{2,1,0:T(8,128)S(1)} reduce-window(s32[32,8,128]{2,1,0:T(8,128)S(1)} %fusion.25, s32[]{:T(128)} %constant.66.clone.1), window={size=1x1x128 pad=0_0x0_0x127_0}, to_apply=%region_0.1 | reduce-window | flops 4161536 | bytes 262148 | tf_op jit(solution)/shard_map/reduce-window
  17.5 0.1 slice.14
  17.6 0.1 copy.16
  17.7 0.1 copy.17
  17.8 0.1 add_add_fusion
  18.0 4.3 %scatter_custom_fusion = s32[512]{0:T(512)S(1)} fusion(s32[1024]{0:T(1024)S(1)} %bitcast.72, s32[1024]{0:T(1024)S(1)} %iota.11, s32[]{:T(128)} %constant.65.clone.1), kind=kCustom, calls=%fused_computation.91 | custom fusion | bytes 2052 | tf_op jit(solution)/shard_map/scatter | solution.py:83
  22.4 0.1 broadcast_in_dim.62
  22.5 38.8 %all_gather.6 = bf16[128,2048]{1,0:T(8,128)(2,1)S(1)} all-gather(bf16[128,128]{1,0:T(8,128)(2,1)} %param.7), channel_id=1, replica_groups=mesh['dp'=32,'expert'=16] {'expert'}, dimensions={1}, use_global_device_ids=true | all-gather | bytes 557056 | tf_op jit(solution)/shard_map/all_gather | solution.py:58
  61.3 2.5 gather_fusion.1
  63.7 1.6 broadcast_select_fusion
  65.3 0.0 copy-start.3
  65.3 7.8 %all-to-all-start = ((bf16[32,16,2048]{2,1,0:T(8,128)(2,1)}), bf16[32,16,2048]{2,1,0:T(8,128)(2,1)}, u32[]{:S(2)}, u32[]{:S(2)}) async-start(bf16[32,16,2048]{2,1,0:T(8,128)(2,1)} %broadcast_select_fusion), calls=%async_computation | async-start | bytes 4194304 | tf_op jit(solution)/shard_map/all_to_all | solution.py:97
  73.1 0.0 copy-done.3
  73.1 0.0 copy-start.2
  73.1 0.1 copy.18
  73.2 0.1 reshape.232
  73.3 2.3 gather_fusion
  75.7 0.1 mul.69
  75.7 0.0 copy-done.2
  75.7 28.7 %all_gather.7 = bf16[128,2048]{1,0:T(8,128)(2,1)S(1)} all-gather(bf16[128,128]{1,0:T(8,128)(2,1)S(1)} %copy-done.2), channel_id=1, replica_groups=mesh['dp'=32,'expert'=16] {'expert'}, dimensions={1}, use_global_device_ids=true | all-gather | bytes 557056 | tf_op jit(solution)/shard_map/all_gather | solution.py:59
  104.5 2.5 gather_fusion.2
  106.9 1.7 fusion
  108.6 0.0 all-to-all-done
  108.6 7.4 %all-to-all-start.2 = ((bf16[32,16,2048]{2,1,0:T(8,128)(2,1)}), bf16[32,16,2048]{2,1,0:T(8,128)(2,1)}, u32[]{:S(2)}, u32[]{:S(2)}) async-start(bf16[32,16,2048]{2,1,0:T(8,128)(2,1)} %fusion), calls=%async_computation.3 | async-start | bytes 4194304 | tf_op jit(solution)/shard_map/all_to_all | solution.py:107
  116.1 0.0 copy-start.1
  116.1 3.4 %fusion.11 = f32[512,192]{0,1:T(8,128)} fusion(bf16[512,2048]{1,0:T(8,128)(2,1)} %bitcast.5, bf16[1,192,2048]{2,1,0:T(8,128)(2,1)} %param.12), kind=kOutput, calls=%fused_computation.27 | convolution fusion | flops 402653184 | bytes 3276800 | tf_op jit(solution)/shard_map/dot_general | solution.py:17
  119.5 0.0 copy-done.1
  119.5 3.2 fusion.15
  122.7 19.4 %all-to-all-done.2 = bf16[32,16,2048]{2,1,0:T(8,128)(2,1)} async-done(((bf16[32,16,2048]{2,1,0:T(8,128)(2,1)}), bf16[32,16,2048]{2,1,0:T(8,128)(2,1)}, u32[]{:S(2)}, u32[]{:S(2)}) %all-to-all-start.2) | async-done | bytes 2097184 | tf_op jit(solution)/shard_map/all_to_all | solution.py:107
  142.1 0.0 copy-done
  142.1 2.7 multiply_convert_fusion
  144.8 2.1 convolution_convert_fusion
  146.8 7.6 %all-to-all-start.1 = ((bf16[32,16,2048]{2,1,0:T(8,128)(2,1)}), bf16[32,16,2048]{2,1,0:T(8,128)(2,1)}, u32[]{:S(2)}, u32[]{:S(2)}) async-start(bf16[32,16,2048]{2,1,0:T(8,128)(2,1)} %bitcast.67), calls=%async_computation.1 | async-start | bytes 4194304 | tf_op jit(solution)/shard_map/all_to_all | solution.py:100
  154.4 0.2 reduce-scatter.3.cloned.1.call-start
  154.7 3.8 %fusion.13 = f32[512,2048]{1,0:T(8,128)} fusion(bf16[512,192]{0,1:T(8,128)(2,1)S(1)} %get-tuple-element.15, bf16[1,192,2048]{2,1,0:T(8,128)(2,1)} %param.11), kind=kOutput, calls=%fused_computation.29 | convolution fusion | flops 402653184 | bytes 5177344 | tf_op jit(solution)/shard_map/dot_general | solution.py:45
  158.5 22.0 %all-to-all-done.1 = bf16[32,16,2048]{2,1,0:T(8,128)(2,1)} async-done(((bf16[32,16,2048]{2,1,0:T(8,128)(2,1)}), bf16[32,16,2048]{2,1,0:T(8,128)(2,1)}, u32[]{:S(2)}, u32[]{:S(2)}) %all-to-all-start.1) | async-done | bytes 2097184 | tf_op jit(solution)/shard_map/all_to_all | solution.py:100
  180.4 3.9 %bitcast_multiply_fusion = f32[512,2048]{1,0:T(8,128)} fusion(f32[512]{0:T(512)S(1)} %broadcast_select_fusion.1, bf16[32,16,2048]{2,1,0:T(8,128)(2,1)} %all-to-all-done.1), kind=kLoop, calls=%fused_computation.13 | loop fusion | flops 2097152 | bytes 6293504 | tf_op jit(solution)/shard_map/mul | solution.py:123
  184.3 9.4 %scatter_custom_fusion.1 = f32[128,2048]{1,0:T(8,128)} fusion(s32[512]{0:T(512)S(1)} %get-tuple-element.18, f32[512,2048]{1,0:T(8,128)} %bitcast_multiply_fusion, f32[]{:T(128)} %constant.64.clone.1), kind=kCustom, calls=%fused_computation.34 | custom fusion | flops 1048576 | bytes 1049088 | tf_op jit(solution)/shard_map/scatter-add | solution.py:123
  193.8 0.0 reduce-scatter.3.cloned.1.call-update
  193.8 0.0 reduce-scatter.5.cloned.1.call-start
  193.8 3.2 add_convert_fusion
  197.0 32.4 %all_to_all.20 = bf16[32,16,2048]{2,1,0:T(8,128)(2,1)} all-to-all(bf16[32,16,2048]{2,1,0:T(8,128)(2,1)S(1)} %bitcast.66), channel_id=1, replica_groups=mesh['dp'=32,'expert'=16] {'dp'}, dimensions={0} | all-to-all | bytes 4194304 | tf_op jit(solution)/shard_map/all_to_all | solution.py:110
  229.4 9.1 %scatter_custom_fusion.2 = f32[128,2048]{1,0:T(8,128)} fusion(s32[512]{0:T(512)S(1)} %get-tuple-element.18, bf16[512,2048]{1,0:T(8,128)(2,1)} %bitcast.68, f32[]{:T(128)} %constant.64.clone.1), kind=kCustom, calls=%fused_computation.11 | custom fusion | flops 2097152 | bytes 3145732 | tf_op jit(solution)/shard_map/scatter-add | solution.py:125
  238.5 0.0 reduce-scatter.5.cloned.1.call-update
  238.6 3.1 fusion.6
  241.6 3.1 fusion.5
  244.7 3.1 fusion.4
  247.8 2.2 fusion.1
  249.9 0.1 reshape.293
  250.0 3.5 %scatter_custom_fusion.3 = f32[1024]{0:T(1024)S(1)} fusion(s32[512]{0:T(512)S(1)} %get-tuple-element.17, f32[512]{0:T(512)S(1)} %reshape.293, f32[]{:T(128)} %constant.64.clone.1), kind=kCustom, calls=%fused_computation.85 | custom fusion | flops 512 | bytes 4100 | tf_op jit(solution)/shard_map/scatter-add | solution.py:130
  253.5 0.1 reshape.237
  253.6 54.9 %psum.7 = f32[128,8]{1,0:T(8,128)S(1)} all-reduce(f32[128,8]{1,0:T(8,128)S(1)} %reshape.237), channel_id=1, replica_groups=mesh['dp'=32,'expert'=16] {'expert'}, use_global_device_ids=true, to_apply=%region_10.11 | all-reduce | flops 1024 | bytes 8192 | tf_op jit(solution)/shard_map/psum | solution.py:137
  308.5 0.7 copy.19
  309.1 0.0 reduce-scatter.3.cloned.1.call-done
  309.1 1.5 convert_element_type.68
  310.6 20.9 %reduce-scatter.5.cloned.1.call-done = f32[128,128]{1,0:T(8,128)} async-done(((f32[128,2048]{1,0:T(8,128)}), f32[128,128]{1,0:T(8,128)}) %reduce-scatter.5.cloned.1.call-update) | async-done | bytes 65552 | tf_op jit(solution)/shard_map/reduce_scatter | solution.py:135
  331.5 1.5 convert_element_type.77
  (15 shorter events, 0.2 us)
Async XLA Ops:
  7.2 134.9 %copy-start = (bf16[1,192,2048]{2,1,0:T(8,128)(2,1)S(1)}, bf16[1,192,2048]{2,1,0:T(8,128)(2,1)}, u32[]{:S(2)}) copy-start(bf16[1,192,2048]{2,1,0:T(8,128)(2,1)} %param.13) | copy-start | bytes 2359300
  65.3 7.8 %copy-start.3 = (f32[128,8]{0,1:T(8,128)S(1)}, f32[128,8]{0,1:T(8,128)}, u32[]{:S(2)}) copy-start(f32[128,8]{0,1:T(8,128)} %param.10) | copy-start | bytes 12292
  65.3 43.3 %all-to-all-start = ((bf16[32,16,2048]{2,1,0:T(8,128)(2,1)}), bf16[32,16,2048]{2,1,0:T(8,128)(2,1)}, u32[]{:S(2)}, u32[]{:S(2)}) async-start(bf16[32,16,2048]{2,1,0:T(8,128)(2,1)} %broadcast_select_fusion), calls=%async_computation | async-start | bytes 4194304 | tf_op jit(solution)/shard_map/all_to_all | solution.py:97
  73.1 2.6 copy-start.2
  108.6 33.4 %all-to-all-start.2 = ((bf16[32,16,2048]{2,1,0:T(8,128)(2,1)}), bf16[32,16,2048]{2,1,0:T(8,128)(2,1)}, u32[]{:S(2)}, u32[]{:S(2)}) async-start(bf16[32,16,2048]{2,1,0:T(8,128)(2,1)} %fusion), calls=%async_computation.3 | async-start | bytes 4194304 | tf_op jit(solution)/shard_map/all_to_all | solution.py:107
  116.1 3.4 %copy-start.1 = (bf16[1,192,2048]{2,1,0:T(8,128)(2,1)S(1)}, bf16[1,192,2048]{2,1,0:T(8,128)(2,1)}, u32[]{:S(2)}) copy-start(bf16[1,192,2048]{2,1,0:T(8,128)(2,1)} %param.11) | copy-start | bytes 2359300
  146.8 33.6 %all-to-all-start.1 = ((bf16[32,16,2048]{2,1,0:T(8,128)(2,1)}), bf16[32,16,2048]{2,1,0:T(8,128)(2,1)}, u32[]{:S(2)}, u32[]{:S(2)}) async-start(bf16[32,16,2048]{2,1,0:T(8,128)(2,1)} %bitcast.67), calls=%async_computation.1 | async-start | bytes 4194304 | tf_op jit(solution)/shard_map/all_to_all | solution.py:100
  154.4 154.7 %reduce-scatter.3.cloned.1.call-start = ((), (), s32[]{:S(2)}) async-start(), calls=%async_computation.6 | async-start | bytes 1114112 | tf_op jit(solution)/shard_map/reduce_scatter | solution.py:134
  193.8 137.7 %reduce-scatter.5.cloned.1.call-start = ((), (), s32[]{:S(2)}) async-start(), calls=%async_computation.7 | async-start | bytes 1114112 | tf_op jit(solution)/shard_map/reduce_scatter | solution.py:135
Sparse Core Ops, SparseCore 0:
  193.9 66.0 reduce-scatter.2
  263.1 68.3 reduce-scatter.4
where the time goes:
time: 341 us; the launch traced here: 340 us
  blocking collectives  155 us (45%)
  waiting for transfers between devices  62.3 us (18%)
  other arithmetic  43.6 us (13%)
  matrix products  27.6 us (8%)
  starting transfers between devices  23.1 us (7%)
  between operations  14.3 us (4%)
  local copies, waits for them, and re-layouts  14.1 us (4%)
    psum x1, blocking collectives, per_device(): grad_gates = lax.psum(gate_part, 'expert')  54.9 us
    all_gather x1, blocking collectives, per_device(): lax.all_gather(tokens, 'expert', axis=1, tiled=True)  38.8 us
    all_to_all x1, blocking collectives, per_device(): lax.all_to_all(part_grad.reshape(dp_count, capacity, features), 'dp', spl...  32.4 us
    all_gather x1, blocking collectives, per_device(): lax.all_gather(cotangent, 'expert', axis=1, tiled=True)  28.7 us
    all_to_all x1, waiting for transfers between devices, per_device(): lax.all_to_all(expert_out.reshape(dp_count, capacity, features), 'dp', sp...  22 us
    reduce_scatter x1, waiting for transfers between devices, per_device(): lax.psum_scatter(grad_part, 'expert', scatter_dimension=1, tiled=True)  20.9 us
    all_to_all x1, waiting for transfers between devices, per_device(): lax.all_to_all(send_do, 'dp', split_axis=0, concat_axis=0, tiled=True)  19.4 us
    scatter-add x1, other arithmetic, per_device(): out_part = jnp.zeros((tok_count, width_now), jnp.float32).at[slot_token]....  9.44 us
  transfers between devices with their start and end apart: 5, of which 3 were waited for; matrix products, arithmetic and copies ran while one was open for 14% of the time, Pallas kernels for 0%

commit v1 on v0

--- a/solution.py
+++ b/solution.py
@@ -54,8 +54,38 @@
 
 
 def per_device(tokens, cotangent, expert_ids, gate_weights, w_gate, w_up, w_down):
+
+    def _settle_set(slab_in, array_axis):
+        all_rows = lax.axis_size("expert")
+        fresh = lax.axis_index("expert")
+        part_now, piece_next, e_now = (all_rows, fresh, slab_in.shape[array_axis])
+        gallery = []
+        for dev_i, no in enumerate(slab_in.shape):
+            gallery.append(no * part_now if dev_i == array_axis else no)
+        newest = lax.dynamic_update_slice_in_dim(
+            jnp.zeros(gallery, slab_in.dtype), slab_in, piece_next * e_now, axis=array_axis
+        )
+        answer = val2 = slab_in
+        for dd in [*range(1, part_now // 2 + 1)]:
+            store = []
+            for dev_i in tuple(range(part_now)):
+                store.append((dev_i, (dev_i + 1) % part_now))
+            answer = lax.ppermute(answer, axis_name="expert", perm=store)
+            newest = lax.dynamic_update_slice_in_dim(
+                newest, answer, (piece_next - dd) % part_now * e_now, axis=array_axis
+            )
+            if 2 * dd < part_now:
+                row_list = []
+                for dev_i in tuple(range(part_now)):
+                    row_list.append((dev_i, (dev_i - 1) % part_now))
+                val2 = lax.ppermute(val2, axis_name="expert", perm=row_list)
+                newest = lax.dynamic_update_slice_in_dim(
+                    newest, val2, (piece_next + dd) % part_now * e_now, axis=array_axis
+                )
+        return newest
+
     full_x, full_dy = (
-        lax.all_gather(tokens, "expert", axis=1, tiled=True),
+        _settle_set(tokens, array_axis=1),
         lax.all_gather(cotangent, "expert", axis=1, tiled=True),
     )
     dp_count = lax.axis_size("dp")

time: 341 us -> 370 us (1.085)
  starting transfers between devices: 23.1 us -> 80.8 us
  blocking collectives: 155 us -> 116 us
  waiting for transfers between devices: 62.3 us -> 70.7 us
    ppermute x0 -> x15, starting transfers between devices: none -> 57.7 us  [the longest x7 42.3 us: _settle_set(): val2 = lax.ppermute(val2, axis_name='expert', perm=row_list)]
    all_gather x1 -> x0, blocking collectives: 38.8 us -> none  [per_device(): lax.all_gather(tokens, 'expert', axis=1, tiled=True)]
    ppermute x0 -> x15, waiting for transfers between devices: none -> 10.1 us  [the longest x8 10.1 us: _settle_set(): answer = lax.ppermute(answer, axis_name='expert', perm=store)]
  transfers between devices with their start and end apart: 5 -> 20, of which waited for: 3 -> 5; matrix products, arithmetic and copies ran while one was open for 14% -> 17% of each run, Pallas kernels for 0% -> 0%
where the time goes in v1:
time: 370 us; the launch traced here: 369 us
  blocking collectives  116 us (31%)
  starting transfers between devices  80.8 us (22%)
  waiting for transfers between devices  70.7 us (19%)
  other arithmetic  43.6 us (12%)
  matrix products  28.4 us (8%)
  between operations  14.9 us (4%)
  local copies, waits for them, and re-layouts  14.4 us (4%)
    psum x1, blocking collectives, per_device(): grad_gates = lax.psum(gate_part, 'expert')  54.8 us
    ppermute x7, starting transfers between devices, _settle_set(): val2 = lax.ppermute(val2, axis_name='expert', perm=row_list)  42.3 us
    all_to_all x1, blocking collectives, per_device(): lax.all_to_all(part_grad.reshape(dp_count, capacity, features), 'dp', spl...  32.4 us
    all_gather x1, blocking collectives, per_device(): lax.all_gather(cotangent, 'expert', axis=1, tiled=True)  28.7 us
    all_to_all x1, waiting for transfers between devices, per_device(): lax.all_to_all(expert_out.reshape(dp_count, capacity, features), 'dp', sp...  21.9 us
    all_to_all x1, waiting for transfers between devices, per_device(): lax.all_to_all(send_do, 'dp', split_axis=0, concat_axis=0, tiled=True)  19.4 us
    reduce_scatter x1, waiting for transfers between devices, per_device(): lax.psum_scatter(grad_part, 'expert', scatter_dimension=1, tiled=True)  19.3 us
    ppermute x8, starting transfers between devices, _settle_set(): answer = lax.ppermute(answer, axis_name='expert', perm=store)  15.4 us
  transfers between devices with their start and end apart: 20, of which 5 were waited for; matrix products, arithmetic and copies ran while one was open for 17% of the time, Pallas kernels for 0%

profile of v1, /device:TPU:2, one launch (start us, length us, event | category | flops | bytes accessed | tf_op | source)
XLA Modules:
  0.0 368.8 jit_solution(7368031509255788481)
XLA Ops:
  7.2 11.5 %collective-permute-start.1 = (bf16[128,128]{1,0:T(8,128)(2,1)}, bf16[128,128]{1,0:T(8,128)(2,1)S(1)}, u32[]{:S(2)}, u32[]{:S(2)}) collective-permute-start(bf16[128,128]{1,0:T(8,128)(2,1)} %param.7), channel_id=1, source_target_pairs={{0,15},{1,0},{2,1},{3,2},{4,3},{5,4},{6,5},{7,6},{8,7},{9,8},{10,9... | collective-permute-start | bytes 98312 | tf_op jit(solution)/shard_map/ppermute | solution.py:81
  18.7 1.9 collective-permute-start
  20.7 0.8 copy.13
  21.5 0.1 reshape.230
  21.5 0.1 reshape.229
  21.6 0.1 reshape.228
  21.9 9.0 %reduce-window.6 = s32[32,8,128]{2,1,0:T(8,128)S(1)} reduce-window(s32[32,8,128]{2,1,0:T(8,128)S(1)} %fusion.25, s32[]{:T(128)} %constant.149.clone.1), window={size=1x1x128 pad=0_0x0_0x127_0}, to_apply=%region_0.1 | reduce-window | flops 4161536 | bytes 262148 | tf_op jit(solution)/shard_map/reduce-window
  30.9 0.1 slice.14
  31.0 0.1 copy.16
  31.2 0.1 add_add_fusion
  31.4 4.3 %scatter_custom_fusion = s32[512]{0:T(512)S(1)} fusion(s32[1024]{0:T(1024)S(1)} %bitcast.72, s32[1024]{0:T(1024)S(1)} %iota.11, s32[]{:T(128)} %constant.148.clone.1), kind=kCustom, calls=%fused_computation.107 | custom fusion | bytes 2052 | tf_op jit(solution)/shard_map/scatter | solution.py:113
  36.1 0.1 broadcast_in_dim.65
  36.2 5.1 %collective-permute-start.3 = (bf16[128,128]{1,0:T(8,128)(2,1)S(1)}, bf16[128,128]{1,0:T(8,128)(2,1)S(1)}, u32[]{:S(2)}, u32[]{:S(2)}) collective-permute-start(bf16[128,128]{1,0:T(8,128)(2,1)S(1)} %collective-permute-done.1), channel_id=1, source_target_pairs={{0,15},{1,0},{2,1},{3,2},{4,3},{5,4},{6,5},{7,6},{8,7},{9,8},{10,9... | collective-permute-start | bytes 98312 | tf_op jit(solution)/shard_map/ppermute | solution.py:81
  41.4 1.9 collective-permute-start.2
  43.4 5.1 %collective-permute-start.5 = (bf16[128,128]{1,0:T(8,128)(2,1)S(1)}, bf16[128,128]{1,0:T(8,128)(2,1)S(1)}, u32[]{:S(2)}, u32[]{:S(2)}) collective-permute-start(bf16[128,128]{1,0:T(8,128)(2,1)S(1)} %collective-permute-done.3), channel_id=1, source_target_pairs={{0,15},{1,0},{2,1},{3,2},{4,3},{5,4},{6,5},{7,6},{8,7},{9,8},{10,9... | collective-permute-start | bytes 98312 | tf_op jit(solution)/shard_map/ppermute | solution.py:81
  48.5 1.9 collective-permute-start.4
  50.5 5.1 %collective-permute-start.7 = (bf16[128,128]{1,0:T(8,128)(2,1)S(1)}, bf16[128,128]{1,0:T(8,128)(2,1)S(1)}, u32[]{:S(2)}, u32[]{:S(2)}) collective-permute-start(bf16[128,128]{1,0:T(8,128)(2,1)S(1)} %collective-permute-done.5), channel_id=1, source_target_pairs={{0,15},{1,0},{2,1},{3,2},{4,3},{5,4},{6,5},{7,6},{8,7},{9,8},{10,9... | collective-permute-start | bytes 98312 | tf_op jit(solution)/shard_map/ppermute | solution.py:81
  55.7 1.9 collective-permute-start.6
  57.7 5.1 %collective-permute-start.9 = (bf16[128,128]{1,0:T(8,128)(2,1)S(1)}, bf16[128,128]{1,0:T(8,128)(2,1)S(1)}, u32[]{:S(2)}, u32[]{:S(2)}) collective-permute-start(bf16[128,128]{1,0:T(8,128)(2,1)S(1)} %collective-permute-done.7), channel_id=1, source_target_pairs={{0,15},{1,0},{2,1},{3,2},{4,3},{5,4},{6,5},{7,6},{8,7},{9,8},{10,9... | collective-permute-start | bytes 98312 | tf_op jit(solution)/shard_map/ppermute | solution.py:81
  62.8 1.9 collective-permute-start.8
  64.8 5.1 %collective-permute-start.11 = (bf16[128,128]{1,0:T(8,128)(2,1)S(1)}, bf16[128,128]{1,0:T(8,128)(2,1)S(1)}, u32[]{:S(2)}, u32[]{:S(2)}) collective-permute-start(bf16[128,128]{1,0:T(8,128)(2,1)S(1)} %collective-permute-done.9), channel_id=1, source_target_pairs={{0,15},{1,0},{2,1},{3,2},{4,3},{5,4},{6,5},{7,6},{8,7},{9,8},{10,9... | collective-permute-start | bytes 98312 | tf_op jit(solution)/shard_map/ppermute | solution.py:81
  69.9 1.9 collective-permute-start.10
  71.9 5.1 %collective-permute-start.13 = (bf16[128,128]{1,0:T(8,128)(2,1)S(1)}, bf16[128,128]{1,0:T(8,128)(2,1)S(1)}, u32[]{:S(2)}, u32[]{:S(2)}) collective-permute-start(bf16[128,128]{1,0:T(8,128)(2,1)S(1)} %collective-permute-done.11), channel_id=1, source_target_pairs={{0,15},{1,0},{2,1},{3,2},{4,3},{5,4},{6,5},{7,6},{8,7},{9,8},{10,9... | collective-permute-start | bytes 98312 | tf_op jit(solution)/shard_map/ppermute | solution.py:81
  77.1 1.9 collective-permute-start.12
  79.1 5.0 %collective-permute-done.12 = bf16[128,128]{1,0:T(8,128)(2,1)S(1)} collective-permute-done((bf16[128,128]{1,0:T(8,128)(2,1)S(1)}, bf16[128,128]{1,0:T(8,128)(2,1)S(1)}, u32[]{:S(2)}, u32[]{:S(2)}) %collective-permute-start.12) | collective-permute-done | bytes 32800 | tf_op jit(solution)/shard_map/ppermute | solution.py:73
  84.1 1.9 collective-permute-start.14
  86.1 5.0 %collective-permute-done.14 = bf16[128,128]{1,0:T(8,128)(2,1)S(1)} collective-permute-done((bf16[128,128]{1,0:T(8,128)(2,1)S(1)}, bf16[128,128]{1,0:T(8,128)(2,1)S(1)}, u32[]{:S(2)}, u32[]{:S(2)}) %collective-permute-start.14) | collective-permute-done | bytes 32800 | tf_op jit(solution)/shard_map/ppermute | solution.py:73
  91.1 2.5 gather_fusion.1
  93.6 1.5 broadcast_select_fusion
  95.1 7.8 %all-to-all-start = ((bf16[32,16,2048]{2,1,0:T(8,128)(2,1)}), bf16[32,16,2048]{2,1,0:T(8,128)(2,1)}, u32[]{:S(2)}, u32[]{:S(2)}) async-start(bf16[32,16,2048]{2,1,0:T(8,128)(2,1)} %broadcast_select_fusion), calls=%async_computation | async-start | bytes 4194304 | tf_op jit(solution)/shard_map/all_to_all | solution.py:127
  103.0 0.1 copy.18
  103.1 0.1 reshape.232
  103.2 2.3 gather_fusion
  105.5 0.1 mul.133
  105.6 28.7 %all_gather.3 = bf16[128,2048]{1,0:T(8,128)(2,1)S(1)} all-gather(bf16[128,128]{1,0:T(8,128)(2,1)S(1)} %copy-done.2), channel_id=1, replica_groups=mesh['dp'=32,'expert'=16] {'expert'}, dimensions={1}, use_global_device_ids=true | all-gather | bytes 557056 | tf_op jit(solution)/shard_map/all_gather | solution.py:89
  134.3 2.5 gather_fusion.2
  136.8 1.7 fusion
  138.5 7.4 %all-to-all-start.2 = ((bf16[32,16,2048]{2,1,0:T(8,128)(2,1)}), bf16[32,16,2048]{2,1,0:T(8,128)(2,1)}, u32[]{:S(2)}, u32[]{:S(2)}) async-start(bf16[32,16,2048]{2,1,0:T(8,128)(2,1)} %fusion), calls=%async_computation.3 | async-start | bytes 4194304 | tf_op jit(solution)/shard_map/all_to_all | solution.py:137
  145.9 3.4 fusion.11
  149.4 3.2 fusion.15
  152.6 19.4 %all-to-all-done.2 = bf16[32,16,2048]{2,1,0:T(8,128)(2,1)} async-done(((bf16[32,16,2048]{2,1,0:T(8,128)(2,1)}), bf16[32,16,2048]{2,1,0:T(8,128)(2,1)}, u32[]{:S(2)}, u32[]{:S(2)}) %all-to-all-start.2) | async-done | bytes 2097184 | tf_op jit(solution)/shard_map/all_to_all | solution.py:137
  171.9 3.4 multiply_convert_fusion
  175.3 2.1 convolution_convert_fusion
  177.3 7.6 %all-to-all-start.1 = ((bf16[32,16,2048]{2,1,0:T(8,128)(2,1)}), bf16[32,16,2048]{2,1,0:T(8,128)(2,1)}, u32[]{:S(2)}, u32[]{:S(2)}) async-start(bf16[32,16,2048]{2,1,0:T(8,128)(2,1)} %bitcast.67), calls=%async_computation.1 | async-start | bytes 4194304 | tf_op jit(solution)/shard_map/all_to_all | solution.py:130
  184.9 0.2 reduce-scatter.3.cloned.1.call-start
  185.2 3.8 %fusion.13 = f32[512,2048]{1,0:T(8,128)} fusion(bf16[512,192]{0,1:T(8,128)(2,1)S(1)} %get-tuple-element.15, bf16[1,192,2048]{2,1,0:T(8,128)(2,1)} %param.11), kind=kOutput, calls=%fused_computation.29 | convolution fusion | flops 402653184 | bytes 5177344 | tf_op jit(solution)/shard_map/dot_general | solution.py:45
  189.0 21.9 %all-to-all-done.1 = bf16[32,16,2048]{2,1,0:T(8,128)(2,1)} async-done(((bf16[32,16,2048]{2,1,0:T(8,128)(2,1)}), bf16[32,16,2048]{2,1,0:T(8,128)(2,1)}, u32[]{:S(2)}, u32[]{:S(2)}) %all-to-all-start.1) | async-done | bytes 2097184 | tf_op jit(solution)/shard_map/all_to_all | solution.py:130
  210.9 3.9 %bitcast_multiply_fusion = f32[512,2048]{1,0:T(8,128)} fusion(f32[512]{0:T(512)S(1)} %broadcast_select_fusion.1, bf16[32,16,2048]{2,1,0:T(8,128)(2,1)} %all-to-all-done.1), kind=kLoop, calls=%fused_computation.13 | loop fusion | flops 2097152 | bytes 6293504 | tf_op jit(solution)/shard_map/mul | solution.py:153
  214.8 9.5 %scatter_custom_fusion.1 = f32[128,2048]{1,0:T(8,128)} fusion(s32[512]{0:T(512)S(1)} %get-tuple-element.18, f32[512,2048]{1,0:T(8,128)} %bitcast_multiply_fusion, f32[]{:T(128)} %constant.147.clone.1), kind=kCustom, calls=%fused_computation.34 | custom fusion | flops 1048576 | bytes 1049088 | tf_op jit(solution)/shard_map/scatter-add | solution.py:153
  224.4 3.2 add_convert_fusion
  227.6 32.4 %all_to_all.20 = bf16[32,16,2048]{2,1,0:T(8,128)(2,1)} all-to-all(bf16[32,16,2048]{2,1,0:T(8,128)(2,1)S(1)} %bitcast.66), channel_id=1, replica_groups=mesh['dp'=32,'expert'=16] {'dp'}, dimensions={0} | all-to-all | bytes 4194304 | tf_op jit(solution)/shard_map/all_to_all | solution.py:140
  260.0 9.1 %scatter_custom_fusion.2 = f32[128,2048]{1,0:T(8,128)} fusion(s32[512]{0:T(512)S(1)} %get-tuple-element.18, bf16[512,2048]{1,0:T(8,128)(2,1)} %bitcast.68, f32[]{:T(128)} %constant.147.clone.1), kind=kCustom, calls=%fused_computation.11 | custom fusion | flops 2097152 | bytes 3145732 | tf_op jit(solution)/shard_map/scatter-add | solution.py:155
  269.1 3.1 fusion.6
  272.2 3.2 fusion.5
  275.4 3.1 fusion.4
  278.4 2.2 fusion.1
  280.6 0.1 reshape.293
  280.7 3.5 scatter_custom_fusion.3
  284.2 0.1 reshape.237
  284.3 54.8 %psum.7 = f32[128,8]{1,0:T(8,128)S(1)} all-reduce(f32[128,8]{1,0:T(8,128)S(1)} %reshape.237), channel_id=1, replica_groups=mesh['dp'=32,'expert'=16] {'expert'}, use_global_device_ids=true, to_apply=%region_10.11 | all-reduce | flops 1024 | bytes 8192 | tf_op jit(solution)/shard_map/psum | solution.py:167
  339.1 0.7 copy.19
  339.8 1.5 convert_element_type.68
  341.2 19.3 %reduce-scatter.5.cloned.1.call-done = f32[128,128]{1,0:T(8,128)} async-done(((f32[128,2048]{1,0:T(8,128)}), f32[128,128]{1,0:T(8,128)}) %reduce-scatter.5.cloned.1.call-update) | async-done | bytes 65552 | tf_op jit(solution)/shard_map/reduce_scatter | solution.py:165
  360.5 1.5 convert_element_type.77
  (61 shorter events, 0.8 us)
Async XLA Ops:
  7.2 164.8 %copy-start = (bf16[1,192,2048]{2,1,0:T(8,128)(2,1)S(1)}, bf16[1,192,2048]{2,1,0:T(8,128)(2,1)}, u32[]{:S(2)}) copy-start(bf16[1,192,2048]{2,1,0:T(8,128)(2,1)} %param.13) | copy-start | bytes 2359300
  7.2 28.6 %copy-start.3 = (bf16[128,128]{1,0:T(8,128)(2,1)S(1)}, bf16[128,128]{1,0:T(8,128)(2,1)}, u32[]{:S(2)}) copy-start(bf16[128,128]{1,0:T(8,128)(2,1)} %param.7) | copy-start | bytes 98308
  7.2 29.0 %collective-permute-start.1 = (bf16[128,128]{1,0:T(8,128)(2,1)}, bf16[128,128]{1,0:T(8,128)(2,1)S(1)}, u32[]{:S(2)}, u32[]{:S(2)}) collective-permute-start(bf16[128,128]{1,0:T(8,128)(2,1)} %param.7), channel_id=1, source_target_pairs={{0,15},{1,0},{2,1},{3,2},{4,3},{5,4},{6,5},{7,6},{8,7},{9,8},{10,9... | collective-permute-start | bytes 98312 | tf_op jit(solution)/shard_map/ppermute | solution.py:81
  18.7 22.7 %collective-permute-start = (bf16[128,128]{1,0:T(8,128)(2,1)}, bf16[128,128]{1,0:T(8,128)(2,1)S(1)}, u32[]{:S(2)}, u32[]{:S(2)}) collective-permute-start(bf16[128,128]{1,0:T(8,128)(2,1)} %param.7), channel_id=1, source_target_pairs={{0,1},{1,2},{2,3},{3,4},{4,5},{5,6},{6,7},{7,8},{8,9},{9,10},{10,1... | collective-permute-start | bytes 98312 | tf_op jit(solution)/shard_map/ppermute | solution.py:73
  36.2 7.1 %collective-permute-start.3 = (bf16[128,128]{1,0:T(8,128)(2,1)S(1)}, bf16[128,128]{1,0:T(8,128)(2,1)S(1)}, u32[]{:S(2)}, u32[]{:S(2)}) collective-permute-start(bf16[128,128]{1,0:T(8,128)(2,1)S(1)} %collective-permute-done.1), channel_id=1, source_target_pairs={{0,15},{1,0},{2,1},{3,2},{4,3},{5,4},{6,5},{7,6},{8,7},{9,8},{10,9... | collective-permute-start | bytes 98312 | tf_op jit(solution)/shard_map/ppermute | solution.py:81
  41.4 7.1 %collective-permute-start.2 = (bf16[128,128]{1,0:T(8,128)(2,1)S(1)}, bf16[128,128]{1,0:T(8,128)(2,1)S(1)}, u32[]{:S(2)}, u32[]{:S(2)}) collective-permute-start(bf16[128,128]{1,0:T(8,128)(2,1)S(1)} %collective-permute-done), channel_id=1, source_target_pairs={{0,1},{1,2},{2,3},{3,4},{4,5},{5,6},{6,7},{7,8},{8,9},{9,10},{10,1... | collective-permute-start | bytes 98312 | tf_op jit(solution)/shard_map/ppermute | solution.py:73
  43.4 7.1 %collective-permute-start.5 = (bf16[128,128]{1,0:T(8,128)(2,1)S(1)}, bf16[128,128]{1,0:T(8,128)(2,1)S(1)}, u32[]{:S(2)}, u32[]{:S(2)}) collective-permute-start(bf16[128,128]{1,0:T(8,128)(2,1)S(1)} %collective-permute-done.3), channel_id=1, source_target_pairs={{0,15},{1,0},{2,1},{3,2},{4,3},{5,4},{6,5},{7,6},{8,7},{9,8},{10,9... | collective-permute-start | bytes 98312 | tf_op jit(solution)/shard_map/ppermute | solution.py:81
  48.5 7.1 %collective-permute-start.4 = (bf16[128,128]{1,0:T(8,128)(2,1)S(1)}, bf16[128,128]{1,0:T(8,128)(2,1)S(1)}, u32[]{:S(2)}, u32[]{:S(2)}) collective-permute-start(bf16[128,128]{1,0:T(8,128)(2,1)S(1)} %collective-permute-done.2), channel_id=1, source_target_pairs={{0,1},{1,2},{2,3},{3,4},{4,5},{5,6},{6,7},{7,8},{8,9},{9,10},{10,1... | collective-permute-start | bytes 98312 | tf_op jit(solution)/shard_map/ppermute | solution.py:73
  50.5 7.1 %collective-permute-start.7 = (bf16[128,128]{1,0:T(8,128)(2,1)S(1)}, bf16[128,128]{1,0:T(8,128)(2,1)S(1)}, u32[]{:S(2)}, u32[]{:S(2)}) collective-permute-start(bf16[128,128]{1,0:T(8,128)(2,1)S(1)} %collective-permute-done.5), channel_id=1, source_target_pairs={{0,15},{1,0},{2,1},{3,2},{4,3},{5,4},{6,5},{7,6},{8,7},{9,8},{10,9... | collective-permute-start | bytes 98312 | tf_op jit(solution)/shard_map/ppermute | solution.py:81
  55.7 7.1 %collective-permute-start.6 = (bf16[128,128]{1,0:T(8,128)(2,1)S(1)}, bf16[128,128]{1,0:T(8,128)(2,1)S(1)}, u32[]{:S(2)}, u32[]{:S(2)}) collective-permute-start(bf16[128,128]{1,0:T(8,128)(2,1)S(1)} %collective-permute-done.4), channel_id=1, source_target_pairs={{0,1},{1,2},{2,3},{3,4},{4,5},{5,6},{6,7},{7,8},{8,9},{9,10},{10,1... | collective-permute-start | bytes 98312 | tf_op jit(solution)/shard_map/ppermute | solution.py:73
  57.7 7.1 %collective-permute-start.9 = (bf16[128,128]{1,0:T(8,128)(2,1)S(1)}, bf16[128,128]{1,0:T(8,128)(2,1)S(1)}, u32[]{:S(2)}, u32[]{:S(2)}) collective-permute-start(bf16[128,128]{1,0:T(8,128)(2,1)S(1)} %collective-permute-done.7), channel_id=1, source_target_pairs={{0,15},{1,0},{2,1},{3,2},{4,3},{5,4},{6,5},{7,6},{8,7},{9,8},{10,9... | collective-permute-start | bytes 98312 | tf_op jit(solution)/shard_map/ppermute | solution.py:81
  62.8 7.1 %collective-permute-start.8 = (bf16[128,128]{1,0:T(8,128)(2,1)S(1)}, bf16[128,128]{1,0:T(8,128)(2,1)S(1)}, u32[]{:S(2)}, u32[]{:S(2)}) collective-permute-start(bf16[128,128]{1,0:T(8,128)(2,1)S(1)} %collective-permute-done.6), channel_id=1, source_target_pairs={{0,1},{1,2},{2,3},{3,4},{4,5},{5,6},{6,7},{7,8},{8,9},{9,10},{10,1... | collective-permute-start | bytes 98312 | tf_op jit(solution)/shard_map/ppermute | solution.py:73
  64.8 7.1 %collective-permute-start.11 = (bf16[128,128]{1,0:T(8,128)(2,1)S(1)}, bf16[128,128]{1,0:T(8,128)(2,1)S(1)}, u32[]{:S(2)}, u32[]{:S(2)}) collective-permute-start(bf16[128,128]{1,0:T(8,128)(2,1)S(1)} %collective-permute-done.9), channel_id=1, source_target_pairs={{0,15},{1,0},{2,1},{3,2},{4,3},{5,4},{6,5},{7,6},{8,7},{9,8},{10,9... | collective-permute-start | bytes 98312 | tf_op jit(solution)/shard_map/ppermute | solution.py:81
  69.9 7.1 %collective-permute-start.10 = (bf16[128,128]{1,0:T(8,128)(2,1)S(1)}, bf16[128,128]{1,0:T(8,128)(2,1)S(1)}, u32[]{:S(2)}, u32[]{:S(2)}) collective-permute-start(bf16[128,128]{1,0:T(8,128)(2,1)S(1)} %collective-permute-done.8), channel_id=1, source_target_pairs={{0,1},{1,2},{2,3},{3,4},{4,5},{5,6},{6,7},{7,8},{8,9},{9,10},{10,1... | collective-permute-start | bytes 98312 | tf_op jit(solution)/shard_map/ppermute | solution.py:73
  71.9 14.1 %collective-permute-start.13 = (bf16[128,128]{1,0:T(8,128)(2,1)S(1)}, bf16[128,128]{1,0:T(8,128)(2,1)S(1)}, u32[]{:S(2)}, u32[]{:S(2)}) collective-permute-start(bf16[128,128]{1,0:T(8,128)(2,1)S(1)} %collective-permute-done.11), channel_id=1, source_target_pairs={{0,15},{1,0},{2,1},{3,2},{4,3},{5,4},{6,5},{7,6},{8,7},{9,8},{10,9... | collective-permute-start | bytes 98312 | tf_op jit(solution)/shard_map/ppermute | solution.py:81
  77.1 7.0 %collective-permute-start.12 = (bf16[128,128]{1,0:T(8,128)(2,1)S(1)}, bf16[128,128]{1,0:T(8,128)(2,1)S(1)}, u32[]{:S(2)}, u32[]{:S(2)}) collective-permute-start(bf16[128,128]{1,0:T(8,128)(2,1)S(1)} %collective-permute-done.10), channel_id=1, source_target_pairs={{0,1},{1,2},{2,3},{3,4},{4,5},{5,6},{6,7},{7,8},{8,9},{9,10},{10,1... | collective-permute-start | bytes 98312 | tf_op jit(solution)/shard_map/ppermute | solution.py:73
  84.1 7.0 %collective-permute-start.14 = (bf16[128,128]{1,0:T(8,128)(2,1)S(1)}, bf16[128,128]{1,0:T(8,128)(2,1)S(1)}, u32[]{:S(2)}, u32[]{:S(2)}) collective-permute-start(bf16[128,128]{1,0:T(8,128)(2,1)S(1)} %collective-permute-done.12), channel_id=1, source_target_pairs={{0,1},{1,2},{2,3},{3,4},{4,5},{5,6},{6,7},{7,8},{8,9},{9,10},{10,1... | collective-permute-start | bytes 98312 | tf_op jit(solution)/shard_map/ppermute | solution.py:73
  95.1 7.8 %copy-start.4 = (f32[128,8]{0,1:T(8,128)S(1)}, f32[128,8]{0,1:T(8,128)}, u32[]{:S(2)}) copy-start(f32[128,8]{0,1:T(8,128)} %param.10) | copy-start | bytes 12292
  95.1 43.3 %all-to-all-start = ((bf16[32,16,2048]{2,1,0:T(8,128)(2,1)}), bf16[32,16,2048]{2,1,0:T(8,128)(2,1)}, u32[]{:S(2)}, u32[]{:S(2)}) async-start(bf16[32,16,2048]{2,1,0:T(8,128)(2,1)} %broadcast_select_fusion), calls=%async_computation | async-start | bytes 4194304 | tf_op jit(solution)/shard_map/all_to_all | solution.py:127
  103.0 2.6 copy-start.2
  138.5 33.4 %all-to-all-start.2 = ((bf16[32,16,2048]{2,1,0:T(8,128)(2,1)}), bf16[32,16,2048]{2,1,0:T(8,128)(2,1)}, u32[]{:S(2)}, u32[]{:S(2)}) async-start(bf16[32,16,2048]{2,1,0:T(8,128)(2,1)} %fusion), calls=%async_computation.3 | async-start | bytes 4194304 | tf_op jit(solution)/shard_map/all_to_all | solution.py:137
  145.9 3.4 copy-start.1
  177.3 33.6 %all-to-all-start.1 = ((bf16[32,16,2048]{2,1,0:T(8,128)(2,1)}), bf16[32,16,2048]{2,1,0:T(8,128)(2,1)}, u32[]{:S(2)}, u32[]{:S(2)}) async-start(bf16[32,16,2048]{2,1,0:T(8,128)(2,1)} %bitcast.67), calls=%async_computation.1 | async-start | bytes 4194304 | tf_op jit(solution)/shard_map/all_to_all | solution.py:130
  184.9 154.8 %reduce-scatter.3.cloned.1.call-start = ((), (), s32[]{:S(2)}) async-start(), calls=%async_computation.6 | async-start | bytes 1114112 | tf_op jit(solution)/shard_map/reduce_scatter | solution.py:164
  224.3 136.2 %reduce-scatter.5.cloned.1.call-start = ((), (), s32[]{:S(2)}) async-start(), calls=%async_computation.7 | async-start | bytes 1114112 | tf_op jit(solution)/shard_map/reduce_scatter | solution.py:165
Sparse Core Ops, SparseCore 0:
  224.4 64.7 reduce-scatter.2
  292.3 68.1 reduce-scatter.4
